TPU v7x, 32 devices: a whole 2x2x4 slice. The times are simulated.
32 devices in a mesh: row: 8 (over z, x), col: 4 (over y, core).
Axes of the slice: x: 2, y: 2, z: 4, core: 2. Of those that a mesh axis runs over, the one named last changes fastest.
Arguments:
- layer_input: bfloat16 [16384, 960], P(('row', 'col')), may hold values from -6 to 6
- norm1_gain: float32 [960], replicated, may hold values from 0.5 to 1.5
- w_qkv: bfloat16 [960, 1600], P('row', 'col'), may hold values from -0.1875 to 0.1875
- w_out: bfloat16 [960, 960], P('row', 'col'), may hold values from -1.5 to 1.5
- norm2_gain: float32 [960], replicated, may hold values from 0.5 to 1.5
- w_gate: bfloat16 [960, 2560], P('row', 'col'), may hold values from -0.1875 to 0.1875
- w_up: bfloat16 [960, 2560], P('row', 'col'), may hold values from -0.1875 to 0.1875
- w_down: bfloat16 [960, 2560], P('row', 'col'), may hold values from -0.15625 to 0.15625
- out_cotangent: bfloat16 [16384, 960], P(('row', 'col')), may hold values from -6 to 6
- seq_lengths: int32 [8, 3], P('row'), may hold values from 1 to 1024, 2048 in all within a row
- position_ids: int32 [16384], P(('row', 'col')), may hold values from 0 to 4094, as said below
- deal_rows: int32 [32, 8], P(('row', 'col')), may hold values from 0 to 7, each once within a row
Outputs:
- layer_output: bfloat16 [16384, 960], P(('row', 'col'))
- grad_input: bfloat16 [16384, 960], P(('row', 'col'))
- grad_norm1: float32 [960], replicated
- grad_qkv: float32 [960, 1600], P('row', 'col')
- grad_out: float32 [960, 960], P('row', 'col')
- grad_norm2: float32 [960], replicated
- grad_gate: float32 [960, 2560], P('row', 'col')
- grad_up: float32 [960, 2560], P('row', 'col')
- grad_down: float32 [960, 2560], P('row', 'col')
Inputs may be any that keep to these rules, and one draw needn't show every extreme that they name: Each row of seq_lengths gives the lengths of the 3 sequences packed in order into one row group of 2048 dealt rows; each row sums to 2048, and its largest entry is exactly 1024. `position_ids`: within each aligned group of 2048 dealt rows the ids start at 0 and rise by 1 or 2 from one row to the next; in some group they rise by 2 at every row. `deal_rows`: each row is a permutation of the 8 row groups.
All inputs are finite; a program needn't handle non-finite values.
Results may differ from a plain program's by a relative error of at most 0.015.
Values may be sent and summed in bfloat16 or wider, within the bound.
A program may use at most 128 MiB of HBM per device.

v0:
```python
import math
import jax
import jax.numpy as jnp
from jax import lax
from jax.sharding import PartitionSpec as P

QUERY_HEADS = 15
KEY_VALUE_HEADS = 5
HEAD_DIMENSION = 64
QUERY_FEATURES = 960
KEY_FEATURES = 320
EPS = 1e-05
NEG_FILL = -1e30
THETA = 10000.0


def matmul(left_mat, right_mat):
    return jnp.dot(left_mat, right_mat, preferred_element_type=jnp.float32)


def matmul_nt(left_mat, right_mat):
    return lax.dot_general(
        left_mat, right_mat, (((1,), (1,)), ((), ())), preferred_element_type=jnp.float32
    )


def matmul_tn(left_mat, right_mat):
    return lax.dot_general(
        left_mat, right_mat, (((0,), (0,)), ((), ())), preferred_element_type=jnp.float32
    )


def rms_scale(values):
    return lax.rsqrt(jnp.mean(values * values, axis=1, keepdims=True) + EPS)


def rope_tables(position, head_size):
    half_size = head_size // 2
    inverse = jnp.exp(
        jnp.arange(half_size, dtype=jnp.float32) * (-2.0 * math.log(THETA) / head_size)
    )
    angles = position.astype(jnp.float32)[:, None] * inverse[None, :]
    return (jnp.cos(angles), jnp.sin(angles))


def apply_rotation(values, cosine_table, sine_table, head_count):
    pieces = values.reshape(values.shape[0], head_count, -1)
    half_size = pieces.shape[2] // 2
    first_half = pieces[:, :, :half_size]
    second_half = pieces[:, :, half_size:]
    cos_wide = cosine_table[:, None, :]
    sin_wide = sine_table[:, None, :]
    turned = jnp.concatenate(
        [
            first_half * cos_wide - second_half * sin_wide,
            second_half * cos_wide + first_half * sin_wide,
        ],
        axis=2,
    )
    return turned.reshape(values.shape)


def reverse_rotation(values, cosine_table, sine_table, head_count):
    pieces = values.reshape(values.shape[0], head_count, -1)
    half_size = pieces.shape[2] // 2
    first_half = pieces[:, :, :half_size]
    second_half = pieces[:, :, half_size:]
    cos_wide = cosine_table[:, None, :]
    sin_wide = sine_table[:, None, :]
    turned = jnp.concatenate(
        [
            first_half * cos_wide + second_half * sin_wide,
            second_half * cos_wide - first_half * sin_wide,
        ],
        axis=2,
    )
    return turned.reshape(values.shape)


def gather_rows(values):
    return lax.all_gather(values, "col", axis=0, tiled=True)


def regroup_tokens(values):
    return lax.all_to_all(values, "col", split_axis=0, concat_axis=1, tiled=True)


def regroup_columns(values):
    return lax.all_to_all(values, "col", split_axis=1, concat_axis=0, tiled=True)


def spread_sum(products, own_rows):
    result = jnp.zeros((lax.axis_size("col") * own_rows, products[0][1].shape[0]), jnp.float32)
    for left_mat, right_mat in products:
        result = result + matmul_nt(left_mat, right_mat)
    return lax.psum_scatter(result, "col", scatter_dimension=0, tiled=True)


def attend(query_heads, heads_of_key, heads_of_value, allowed, factor):
    heads_per_group = query_heads.shape[0] // heads_of_key.shape[0]

    def one_head(unused, element):
        query_rows, head_index = element
        key_rows = lax.dynamic_index_in_dim(
            heads_of_key, head_index // heads_per_group, 0, keepdims=False
        )
        value_rows = lax.dynamic_index_in_dim(
            heads_of_value, head_index // heads_per_group, 0, keepdims=False
        )
        scores = jnp.where(allowed, matmul_nt(query_rows, key_rows) * factor, NEG_FILL)
        row_max = jnp.max(scores, axis=1, keepdims=True)
        weights = jnp.exp(scores - row_max)
        row_total = jnp.sum(weights, axis=1, keepdims=True)
        prob_low = (weights / row_total).astype(jnp.bfloat16)
        logsum = row_max[:, 0] + jnp.log(row_total[:, 0])
        return (unused, (matmul(prob_low, value_rows), logsum))

    head_ids = jnp.arange(query_heads.shape[0], dtype=jnp.int32)
    ignored, (head_outputs, logsum) = lax.scan(
        one_head, jnp.zeros((), jnp.float32), (query_heads, head_ids)
    )
    return (head_outputs, logsum)


def attend_back(query_heads, heads_of_key, heads_of_value, grad_heads, logsum, allowed, factor):
    heads_per_group = query_heads.shape[0] // heads_of_key.shape[0]

    def one_head(state, element):
        key_acc, value_acc = state
        query_rows, grad_rows, head_sum, head_index = element
        kv_index = head_index // heads_per_group
        key_rows = lax.dynamic_index_in_dim(heads_of_key, kv_index, 0, keepdims=False)
        value_rows = lax.dynamic_index_in_dim(heads_of_value, kv_index, 0, keepdims=False)
        scores = jnp.where(allowed, matmul_nt(query_rows, key_rows) * factor, NEG_FILL)
        probs = jnp.exp(scores - head_sum[:, None])
        prob_grad = matmul_nt(grad_rows, value_rows)
        score_grad = (
            probs * (prob_grad - jnp.sum(probs * prob_grad, axis=1, keepdims=True))
        ).astype(jnp.bfloat16)
        query_grad = matmul(score_grad, key_rows) * factor
        key_grad = matmul_tn(score_grad, query_rows) * factor
        value_grad = matmul_tn(probs.astype(jnp.bfloat16), grad_rows)
        key_acc = lax.dynamic_update_index_in_dim(
            key_acc,
            lax.dynamic_index_in_dim(key_acc, kv_index, 0, keepdims=False) + key_grad,
            kv_index,
            0,
        )
        value_acc = lax.dynamic_update_index_in_dim(
            value_acc,
            lax.dynamic_index_in_dim(value_acc, kv_index, 0, keepdims=False) + value_grad,
            kv_index,
            0,
        )
        return ((key_acc, value_acc), query_grad)

    head_ids = jnp.arange(query_heads.shape[0], dtype=jnp.int32)
    empty = jnp.zeros(heads_of_key.shape, jnp.float32)
    (key_acc, value_acc), query_grads = lax.scan(
        one_head, (empty, empty), (query_heads, grad_heads, logsum, head_ids)
    )
    return (query_grads, key_acc, value_acc)


def on_device(
    layer_input,
    norm1_gain,
    w_qkv,
    w_out,
    norm2_gain,
    w_gate,
    w_up,
    w_down,
    out_cotangent,
    seq_lengths,
    position_ids,
    deal_rows,
):
    own_rows, model_width = layer_input.shape
    row_devices = lax.axis_size("row")
    col_devices = lax.axis_size("col")
    block_rows = own_rows // row_devices
    rows_per_group = own_rows * col_devices
    row_ids = jnp.arange(row_devices, dtype=jnp.int32)
    targets = deal_rows[0]
    sender = jnp.sum(jnp.where(targets[:, None] == row_ids[None, :], row_ids[:, None], 0), axis=0)
    input_blocks = jnp.take(
        layer_input.reshape(row_devices, block_rows, model_width), sender, axis=0
    ).reshape(own_rows, model_width)
    cot_blocks = jnp.take(
        out_cotangent.reshape(row_devices, block_rows, model_width), sender, axis=0
    ).reshape(own_rows, model_width)
    dealt_input, dealt_cot = (
        lax.all_to_all(input_blocks, "row", split_axis=0, concat_axis=0, tiled=True),
        lax.all_to_all(cot_blocks, "row", split_axis=0, concat_axis=0, tiled=True),
    )
    qkv_mat, out_mat, gate_mat, up_mat, down_mat = (
        lax.all_gather(w_qkv, "row", axis=0, tiled=True),
        lax.all_gather(w_out, "row", axis=0, tiled=True),
        lax.all_gather(w_gate, "row", axis=0, tiled=True),
        lax.all_gather(w_up, "row", axis=0, tiled=True),
        lax.all_gather(w_down, "row", axis=0, tiled=True),
    )
    inputs_f = dealt_input.astype(jnp.float32)
    scale_one = rms_scale(inputs_f)
    normed_one = inputs_f * scale_one
    xn_one = (normed_one * norm1_gain).astype(jnp.bfloat16)
    xn_one_rows = gather_rows(xn_one)
    query_key_value_local = regroup_tokens(matmul(xn_one_rows, qkv_mat).astype(jnp.bfloat16))
    factor = 1.0 / math.sqrt(HEAD_DIMENSION)
    cosine_table, sine_table = rope_tables(position_ids, HEAD_DIMENSION)
    query_r = apply_rotation(
        query_key_value_local[:, :QUERY_FEATURES].astype(jnp.float32),
        cosine_table,
        sine_table,
        QUERY_HEADS,
    ).astype(jnp.bfloat16)
    key_repeated = apply_rotation(
        query_key_value_local[:, QUERY_FEATURES : QUERY_FEATURES + KEY_FEATURES].astype(
            jnp.float32
        ),
        cosine_table,
        sine_table,
        KEY_VALUE_HEADS,
    ).astype(jnp.bfloat16)
    value_own = query_key_value_local[:, QUERY_FEATURES + KEY_FEATURES :]
    key_full, value_full = (
        lax.all_gather(key_repeated, "col", axis=0, tiled=True),
        lax.all_gather(value_own, "col", axis=0, tiled=True),
    )
    col_index = lax.axis_index("col")
    key_ids = jnp.arange(rows_per_group, dtype=jnp.int32)
    query_ids = col_index * own_rows + jnp.arange(own_rows, dtype=jnp.int32)
    bounds = jnp.cumsum(seq_lengths[0])
    key_seg = jnp.sum((key_ids[:, None] >= bounds[None, :]).astype(jnp.int32), axis=1)
    query_seg = jnp.sum((query_ids[:, None] >= bounds[None, :]).astype(jnp.int32), axis=1)
    allowed = (query_seg[:, None] == key_seg[None, :]) & (key_ids[None, :] <= query_ids[:, None])
    query_heads = query_r.reshape(own_rows, QUERY_HEADS, HEAD_DIMENSION).transpose(1, 0, 2)
    heads_of_key = key_full.reshape(rows_per_group, KEY_VALUE_HEADS, HEAD_DIMENSION).transpose(
        1, 0, 2
    )
    heads_of_value = value_full.reshape(rows_per_group, KEY_VALUE_HEADS, HEAD_DIMENSION).transpose(
        1, 0, 2
    )
    head_outputs, logsum = attend(query_heads, heads_of_key, heads_of_value, allowed, factor)
    attn_own = (
        head_outputs.transpose(1, 0, 2).reshape(own_rows, QUERY_FEATURES).astype(jnp.bfloat16)
    )
    attn_cols = regroup_columns(attn_own)
    attn_proj = spread_sum(((attn_cols, out_mat),), own_rows)
    residual = inputs_f + attn_proj
    scale_two = rms_scale(residual)
    normed_two = residual * scale_two
    xn_two = (normed_two * norm2_gain).astype(jnp.bfloat16)
    xn_two_rows = gather_rows(xn_two)
    gate_pre = matmul(xn_two_rows, gate_mat)
    up_pre = matmul(xn_two_rows, up_mat)
    sigmoid_gate = jax.nn.sigmoid(gate_pre)
    hidden = (gate_pre * sigmoid_gate * up_pre).astype(jnp.bfloat16)
    mlp_proj = spread_sum(((hidden, down_mat),), own_rows)
    layer_out = (residual + mlp_proj).astype(jnp.bfloat16)
    cot_f = dealt_cot.astype(jnp.float32)
    cot_rows = gather_rows(dealt_cot)
    hidden_grad = matmul(cot_rows, down_mat)
    grad_down_part = matmul_tn(cot_rows, hidden)
    gate_grad = (
        hidden_grad * up_pre * sigmoid_gate * (1.0 + gate_pre * (1.0 - sigmoid_gate))
    ).astype(jnp.bfloat16)
    up_grad = (hidden_grad * gate_pre * sigmoid_gate).astype(jnp.bfloat16)
    xn_two_grad = spread_sum(((gate_grad, gate_mat), (up_grad, up_mat)), own_rows)
    grad_gate_part = matmul_tn(xn_two_rows, gate_grad)
    grad_up_part = matmul_tn(xn_two_rows, up_grad)
    gain_two_part = jnp.sum(xn_two_grad * normed_two, axis=0)
    normed_grad = xn_two_grad * norm2_gain
    residual_grad = cot_f + scale_two * (
        normed_grad - normed_two * jnp.mean(normed_grad * normed_two, axis=1, keepdims=True)
    )
    branch_grad = residual_grad.astype(jnp.bfloat16)
    branch_rows = gather_rows(branch_grad)
    attn_grad = regroup_tokens(matmul(branch_rows, out_mat).astype(jnp.bfloat16))
    grad_out_part = matmul_tn(branch_rows, attn_cols)
    grad_heads = attn_grad.reshape(own_rows, QUERY_HEADS, HEAD_DIMENSION).transpose(1, 0, 2)
    query_grads, key_acc, value_acc = attend_back(
        query_heads, heads_of_key, heads_of_value, grad_heads, logsum, allowed, factor
    )
    key_part = key_acc.transpose(1, 0, 2).reshape(rows_per_group, KEY_FEATURES)
    value_part = value_acc.transpose(1, 0, 2).reshape(rows_per_group, KEY_FEATURES)
    key_backward, value_back = (
        lax.psum_scatter(
            key_part.astype(jnp.bfloat16), "col", scatter_dimension=0, tiled=True
        ).astype(jnp.float32),
        lax.psum_scatter(
            value_part.astype(jnp.bfloat16), "col", scatter_dimension=0, tiled=True
        ).astype(jnp.float32),
    )
    query_back = reverse_rotation(
        query_grads.transpose(1, 0, 2).reshape(own_rows, QUERY_FEATURES),
        cosine_table,
        sine_table,
        QUERY_HEADS,
    )
    key_rotated = reverse_rotation(key_backward, cosine_table, sine_table, KEY_VALUE_HEADS)
    qkv_grad = jnp.concatenate([query_back, key_rotated, value_back], axis=1).astype(jnp.bfloat16)
    qkv_cols = regroup_columns(qkv_grad)
    xn_one_grad = spread_sum(((qkv_cols, qkv_mat),), own_rows)
    grad_qkv_part = matmul_tn(xn_one_rows, qkv_cols)
    gain_one_part = jnp.sum(xn_one_grad * normed_one, axis=0)
    normed_grad_one = xn_one_grad * norm1_gain
    input_grad = residual_grad + scale_one * (
        normed_grad_one - normed_one * jnp.mean(normed_grad_one * normed_one, axis=1, keepdims=True)
    )
    grad_qkv, grad_out, grad_gate, grad_up, grad_down = (
        lax.psum_scatter(grad_qkv_part, "row", scatter_dimension=0, tiled=True),
        lax.psum_scatter(grad_out_part, "row", scatter_dimension=0, tiled=True),
        lax.psum_scatter(grad_gate_part, "row", scatter_dimension=0, tiled=True),
        lax.psum_scatter(grad_up_part, "row", scatter_dimension=0, tiled=True),
        lax.psum_scatter(grad_down_part, "row", scatter_dimension=0, tiled=True),
    )
    grad_norm1, grad_norm2 = lax.psum((gain_one_part, gain_two_part), ("row", "col"))
    back_out, back_grad = (
        lax.all_to_all(layer_out, "row", split_axis=0, concat_axis=0, tiled=True),
        lax.all_to_all(
            input_grad.astype(jnp.bfloat16), "row", split_axis=0, concat_axis=0, tiled=True
        ),
    )
    layer_output = jnp.take(
        back_out.reshape(row_devices, block_rows, model_width), targets, axis=0
    ).reshape(own_rows, model_width)
    grad_input = jnp.take(
        back_grad.reshape(row_devices, block_rows, model_width), targets, axis=0
    ).reshape(own_rows, model_width)
    return (
        layer_output,
        grad_input,
        grad_norm1,
        grad_qkv,
        grad_out,
        grad_norm2,
        grad_gate,
        grad_up,
        grad_down,
    )


def solution(mesh):
    placed = (
        P(("row", "col"), None),
        P(),
        P("row", "col"),
        P("row", "col"),
        P(),
        P("row", "col"),
        P("row", "col"),
        P("row", "col"),
        P(("row", "col"), None),
        P("row", None),
        P(("row", "col")),
        P(("row", "col"), None),
    )
    return jax.shard_map(
        on_device,
        mesh=mesh,
        in_specs=placed,
        out_specs=(
            P(("row", "col"), None),
            P(("row", "col"), None),
            P(),
            P("row", "col"),
            P("row", "col"),
            P(),
            P("row", "col"),
            P("row", "col"),
            P("row", "col"),
        ),
        check_vma=False,
    )
```

profile of v0, /device:TPU:0, one launch (start us, length us, event | category | flops | bytes accessed | tf_op | source)
XLA Modules:
  0.0 1575.9 jit_solution(9520040302750912809)
XLA Ops:
  13.4 32.9 %all_to_all.100 = bf16[8,64,960]{2,1,0:T(8,128)(2,1)S(1)} all-to-all(bf16[8,64,960]{2,1,0:T(8,128)(2,1)S(1)} %get-tuple-element.545), channel_id=1, replica_groups=mesh['row'=8,'col'=4] {'row'}, dimensions={0} | all-to-all | bytes 1966080 | tf_op jit(solution)/shard_map/all_to_all | solution.py:194
  48.7 32.4 %all-gather = bf16[8,120,400]{1,2,0:T(8,128)(2,1)S(1)} all-gather(bf16[1,120,400]{1,2,0:T(8,128)(2,1)S(1)} %bitcast.267), channel_id=1, replica_groups=mesh['row'=8,'col'=4] {'row'}, dimensions={0}, use_global_device_ids=true | all-gather | bytes 864000 | tf_op jit(solution)/shard_map/all_gather | solution.py:198
  82.8 4.2 convolution_convert_fusion
  88.4 4.4 all-to-all-start.1
  93.2 20.4 %all-to-all-done.1 = bf16[4,512,400]{1,2,0:T(8,128)(2,1)} async-done(((bf16[4,512,400]{1,2,0:T(8,128)(2,1)}), bf16[4,512,400]{1,2,0:T(8,128)(2,1)}, u32[]{:S(2)}, u32[]{:S(2)}) %all-to-all-start.1) | async-done | bytes 1638432 | tf_op jit(solution)/shard_map/all_to_all | solution.py:85
  122.2 10.6 all-gather.13.cloned.1.call-done
  132.8 3.8 copy.90
  136.6 16.6 %all-gather.15.cloned.1.call-done = bf16[2048,320]{0,1:T(8,128)(2,1)} async-done(((bf16[512,320]{0,1:T(8,128)(2,1)}), bf16[2048,320]{0,1:T(8,128)(2,1)}) %all-gather.15.cloned.1.call-update) | async-done | bytes 1310736 | tf_op jit(solution)/shard_map/all_gather | solution.py:229
  153.1 3.8 copy.91
  156.9 146.1 %while.34 = (s32[]{:T(128)}, bf16[15,512,64]{1,2,0:T(8,128)(2,1)}, f32[15,512]{1,0:T(8,128)}, bf16[15,512,64]{2,1,0:T(8,128)(2,1)}, s32[15]{0:T(128)S(1)}, /*ind...) while((s32[]{:T(128)}, bf16[15,512,64]{1,2,0:T(8,128)(2,1)}, ...), condition=%wide.region_8.10_spmd.clone.clone, body=%wide.region_5.9_spmd.clone.sunk.clone | while | flops 279969280 | bytes 13926677 | solution.py:119
  303.0 3.5 all-to-all-start.2
  306.6 31.5 %all_gather.37 = bf16[960,240]{1,0:T(8,128)(2,1)S(1)} all-gather(bf16[120,240]{1,0:T(8,128)(2,1)S(1)} %copy-done.24), channel_id=1, replica_groups=mesh['row'=8,'col'=4] {'row'}, dimensions={0}, use_global_device_ids=true | all-gather | bytes 518400 | tf_op jit(solution)/shard_map/all_gather | solution.py:199
  339.1 4.3 fusion.59
  344.3 69.5 %reduce-scatter.20.cloned.1.call-done = f32[512,960]{0,1:T(8,128)} async-done(((f32[2048,960]{0,1:T(8,128)}), f32[512,960]{0,1:T(8,128)}) %reduce-scatter.20.cloned.1.call-update) | async-done | bytes 1966096 | tf_op jit(solution)/shard_map/reduce_scatter | solution.py:96
  419.7 31.2 %all_to_all.101 = bf16[8,64,960]{2,1,0:T(8,128)(2,1)} all-to-all(bf16[8,64,960]{2,1,0:T(8,128)(2,1)S(1)} %copy-done.8), channel_id=1, replica_groups=mesh['row'=8,'col'=4] {'row'}, dimensions={0} | all-to-all | bytes 1966080 | tf_op jit(solution)/shard_map/all_to_all | solution.py:195
  451.3 8.3 fusion.50
  459.6 35.7 %all-gather.19.cloned.1.call-done = bf16[960,640]{1,0:T(8,128)(2,1)} async-done(((bf16[120,640]{1,0:T(8,128)(2,1)}), bf16[960,640]{1,0:T(8,128)(2,1)}) %all-gather.19.cloned.1.call-update) | async-done | bytes 1228816 | tf_op jit(solution)/shard_map/all_gather | solution.py:200
  495.3 8.3 fusion.49
  503.6 34.6 %all-gather.23.cloned.1.call-done = bf16[960,640]{1,0:T(8,128)(2,1)} async-done(((bf16[120,640]{1,0:T(8,128)(2,1)}), bf16[960,640]{1,0:T(8,128)(2,1)}) %all-gather.23.cloned.1.call-update) | async-done | bytes 1228816 | tf_op jit(solution)/shard_map/all_gather | solution.py:202
  538.2 34.7 %all-gather.25.cloned.1.call-done = bf16[2048,960]{1,0:T(8,128)(2,1)} async-done(((bf16[512,960]{1,0:T(8,128)(2,1)}), bf16[2048,960]{1,0:T(8,128)(2,1)}) %all-gather.25.cloned.1.call-update) | async-done | bytes 3932176 | tf_op jit(solution)/shard_map/all_gather | solution.py:81
  572.9 10.5 multiply_convert_fusion.1
  586.7 5.4 convolution_add_fusion.1
  594.6 66.5 %reduce-scatter.24.cloned.1.call-done = f32[512,960]{0,1:T(8,128)} async-done(((f32[2048,960]{0,1:T(8,128)}), f32[512,960]{0,1:T(8,128)}) %reduce-scatter.24.cloned.1.call-update) | async-done | bytes 1966096 | tf_op jit(solution)/shard_map/reduce_scatter | solution.py:96
  664.9 33.2 %all-gather.27.cloned.1.call-done = bf16[2048,960]{0,1:T(8,128)(2,1)} async-done(((bf16[512,960]{0,1:T(8,128)(2,1)}), bf16[2048,960]{0,1:T(8,128)(2,1)}) %all-gather.27.cloned.1.call-update) | async-done | bytes 3932176 | tf_op jit(solution)/shard_map/all_gather | solution.py:81
  706.0 13.7 all-to-all-done.5
  722.7 236.6 %while.35 = (s32[]{:T(128)}, f32[5,2048,64]{1,2,0:T(8,128)}, f32[5,2048,64]{1,2,0:T(8,128)S(1)}, f32[15,512,64]{1,2,0:T(8,128)}, s32[15]{0:T(128)S(1)}, /*index=...) while((s32[]{:T(128)}, f32[5,2048,64]{1,2,0:T(8,128)}, ...), condition=%wide.region_16.18_spmd.clone.clone, body=%wide.region_14.17_spmd.clone.sunk.clone | while | flops 684097024 | bytes 37771592 | solution.py:159
  965.7 23.3 %reduce-scatter.26.cloned.1.call-done = bf16[512,320]{0,1:T(8,128)(2,1)} async-done(((bf16[2048,320]{0,1:T(8,128)(2,1)}), bf16[512,320]{0,1:T(8,128)(2,1)}) %reduce-scatter.26.cloned.1.call-update) | async-done | bytes 327696 | tf_op jit(solution)/shard_map/reduce_scatter | solution.py:289
  990.2 28.1 %reduce-scatter.28.cloned.1.call-done = bf16[512,320]{0,1:T(8,128)(2,1)} async-done(((bf16[2048,320]{0,1:T(8,128)(2,1)}), bf16[512,320]{0,1:T(8,128)(2,1)}) %reduce-scatter.28.cloned.1.call-update) | async-done | bytes 327696 | tf_op jit(solution)/shard_map/reduce_scatter | solution.py:292
  1019.4 23.3 %all_to_all.102 = bf16[512,4,400]{0,2,1:T(8,128)(2,1)S(1)} all-to-all(bf16[512,4,400]{0,2,1:T(8,128)(2,1)S(1)} %bitcast.241), channel_id=1, replica_groups=mesh['row'=8,'col'=4] {'col'}, dimensions={1} | all-to-all | bytes 3276800 | tf_op jit(solution)/shard_map/all_to_all | solution.py:89
  1043.0 5.3 fusion.53
  1049.6 7.9 fusion.51
  1057.6 6.5 fusion.54
  1064.4 7.9 fusion.58
  1072.4 7.9 fusion.56
  1080.4 6.8 fusion.57
  1087.2 30.1 %reduce-scatter.30.cloned.1.call-done = f32[512,960]{0,1:T(8,128)} async-done(((f32[2048,960]{0,1:T(8,128)}), f32[512,960]{0,1:T(8,128)}) %reduce-scatter.30.cloned.1.call-update) | async-done | bytes 1966096 | tf_op jit(solution)/shard_map/reduce_scatter | solution.py:96
  1119.5 69.3 %reduce-scatter.22.cloned.1.call-done = f32[512,960]{0,1:T(8,128)} async-done(((f32[2048,960]{0,1:T(8,128)}), f32[512,960]{0,1:T(8,128)}) %reduce-scatter.22.cloned.1.call-update) | async-done | bytes 1966096 | tf_op jit(solution)/shard_map/reduce_scatter | solution.py:96
  1188.8 4.7 add_convert_fusion
  1195.9 5.6 all-to-all-start.7
  1202.9 38.0 %all-to-all-done.7 = bf16[8,64,960]{2,1,0:T(8,128)(2,1)S(1)} async-done(((bf16[8,64,960]{2,1,0:T(8,128)(2,1)}), bf16[8,64,960]{2,1,0:T(8,128)(2,1)S(1)}, u32[]{:S(2)}, u32[]{:S(2)}) %all-to-all-start.7) | async-done | bytes 983072 | tf_op jit(solution)/shard_map/all_to_all | solution.py:322
  1240.8 3.6 all-to-all-start.3
  1244.5 4.4 fusion.55
  1248.9 31.4 %reduce-scatter.34.cloned.1.call-done = f32[120,400]{1,0:T(8,128)} async-done(((f32[960,400]{1,0:T(8,128)}), f32[120,400]{1,0:T(8,128)}) %reduce-scatter.34.cloned.1.call-update) | async-done | bytes 192016
  1282.1 39.7 %all-reduce.3 = (f32[960]{0:T(1024)}, f32[960]{0:T(1024)}) all-reduce(f32[960]{0:T(1024)S(1)} %get-tuple-element.467, f32[960]{0:T(1024)S(1)} %get-tuple-element.465), channel_id=1, replica_groups=mesh['row'=8,'col'=4] {'row','col'}, use_global_device_ids=true, to_apply=%region_22.24 | all-reduce | flops 1920 | bytes 15360 | tf_op jit(solution)/shard_map/psum | solution.py:319
  1327.9 26.9 %reduce-scatter.40.cloned.1.call-done = f32[120,640]{1,0:T(8,128)} async-done(((f32[960,640]{1,0:T(8,128)}), f32[120,640]{1,0:T(8,128)}) %reduce-scatter.40.cloned.1.call-update) | async-done | bytes 307216
  1354.8 73.3 %reduce-scatter.36.cloned.1.call-done = f32[120,640]{1,0:T(8,128)} async-done(((f32[960,640]{1,0:T(8,128)}), f32[120,640]{1,0:T(8,128)}) %reduce-scatter.36.cloned.1.call-update) | async-done | bytes 307216
  1428.1 73.4 %reduce-scatter.38.cloned.1.call-done = f32[120,640]{1,0:T(8,128)} async-done(((f32[960,640]{1,0:T(8,128)}), f32[120,640]{1,0:T(8,128)}) %reduce-scatter.38.cloned.1.call-update) | async-done | bytes 307216
  1501.5 66.6 %reduce-scatter.32.cloned.1.call-done = f32[120,240]{1,0:T(8,128)} async-done(((f32[960,240]{1,0:T(8,128)}), f32[120,240]{1,0:T(8,128)}) %reduce-scatter.32.cloned.1.call-update) | async-done | bytes 115216 | tf_op jit(solution)/shard_map/reduce_scatter | solution.py:314
  (414 shorter events, 395.2 us)
Async XLA Ops:
  8.0 74.8 %all-gather.11.cloned.1.call-start = ((), (), s32[]{:S(2)}) async-start(), calls=%async_computation.19 | async-start | bytes 4915200 | tf_op jit(solution)/shard_map/all_gather | solution.py:81
  13.4 33.8 %copy-start.25 = (f32[960]{0:T(1024)S(1)}, f32[960]{0:T(1024)}, u32[]{:S(2)}) copy-start(f32[960]{0:T(1024)} %param.19) | copy-start | bytes 11524
  47.3 366.5 %copy-start = (f32[512,960]{0,1:T(8,128)}, f32[512,960]{0,1:T(8,128)S(1)}, u32[]{:S(2)}) copy-start(f32[512,960]{0,1:T(8,128)S(1)} %copy.93) | copy-start | bytes 5898244
  87.0 5.8 copy-start.29
  88.4 25.2 %all-to-all-start.1 = ((bf16[4,512,400]{1,2,0:T(8,128)(2,1)}), bf16[4,512,400]{1,2,0:T(8,128)(2,1)}, u32[]{:S(2)}, u32[]{:S(2)}) async-start(bf16[4,512,400]{1,2,0:T(8,128)(2,1)} %bitcast.240), calls=%async_computation.1 | async-start | bytes 3276800 | tf_op jit(solution)/shard_map/all_to_all | solution.py:85
  92.7 24.4 %copy-start.32 = (s32[1,3]{1,0:T(1,128)S(1)}, s32[1,3]{1,0:T(1,128)}, u32[]{:S(2)}) copy-start(s32[1,3]{1,0:T(1,128)} %param.27) | copy-start | bytes 40
  92.7 40.0 %all-gather.13.cloned.1.call-start = ((), (), s32[]{:S(2)}) async-start(), calls=%async_computation.20 | async-start | bytes 1638400 | tf_op jit(solution)/shard_map/all_gather | solution.py:228
  93.1 26.9 %copy-start.15 = (f32[512,32]{0,1:T(8,128)}, f32[512,32]{0,1:T(8,128)S(1)}, u32[]{:S(2)}) copy-start(f32[512,32]{0,1:T(8,128)S(1)} %get-tuple-element.540) | copy-start | bytes 196612
  93.2 26.9 %copy-start.17 = (f32[512,32]{0,1:T(8,128)}, f32[512,32]{0,1:T(8,128)S(1)}, u32[]{:S(2)}) copy-start(f32[512,32]{0,1:T(8,128)S(1)} %get-tuple-element.541) | copy-start | bytes 196612
  116.4 36.8 %all-gather.15.cloned.1.call-start = ((), (), s32[]{:S(2)}) async-start(), calls=%async_computation.21 | async-start | bytes 1638400 | tf_op jit(solution)/shard_map/all_gather | solution.py:229
  156.9 149.7 %copy-start.24 = (bf16[120,240]{1,0:T(8,128)(2,1)S(1)}, bf16[120,240]{1,0:T(8,128)(2,1)}, u32[]{:S(2)}) copy-start(bf16[120,240]{1,0:T(8,128)(2,1)} %param.21) | copy-start | bytes 172804
  303.0 35.1 %all-to-all-start.2 = ((bf16[512,4,240]{0,2,1:T(8,128)(2,1)}), bf16[512,4,240]{0,2,1:T(8,128)(2,1)S(1)}, u32[]{:S(2)}, u32[]{:S(2)}) async-start(bf16[512,4,240]{0,2,1:T(8,128)(2,1)} %bitcast.20), calls=%async_computation.2 | async-start | bytes 1966080 | tf_op jit(solution)/shard_map/all_to_all | solution.py:89
  306.5 107.3 %reduce-scatter.20.cloned.1.call-start = ((), (), s32[]{:S(2)}) async-start(), calls=%async_computation.22 | async-start | bytes 9830400 | tf_op jit(solution)/shard_map/reduce_scatter | solution.py:96
  343.4 107.5 %all-gather.21.cloned.1.call-start = ((), (), s32[]{:S(2)}) async-start(), calls=%async_computation.25 | async-start | bytes 1382400 | tf_op jit(solution)/shard_map/all_gather | solution.py:201
  344.0 73.1 %copy-start.23 = (f32[960]{0:T(1024)S(1)}, f32[960]{0:T(1024)}, u32[]{:S(2)}) copy-start(f32[960]{0:T(1024)} %param.22) | copy-start | bytes 11524
  344.0 107.2 %all-gather.17.cloned.1.call-start = ((), (), s32[]{:S(2)}) async-start(), calls=%async_computation.23 | async-start | bytes 4915200 | tf_op jit(solution)/shard_map/all_gather | solution.py:81
  415.8 4.0 copy-start.8
  418.3 76.9 %all-gather.19.cloned.1.call-start = ((), (), s32[]{:S(2)}) async-start(), calls=%async_computation.24 | async-start | bytes 1382400 | tf_op jit(solution)/shard_map/all_gather | solution.py:200
  418.9 119.2 %all-gather.23.cloned.1.call-start = ((), (), s32[]{:S(2)}) async-start(), calls=%async_computation.26 | async-start | bytes 1382400 | tf_op jit(solution)/shard_map/all_gather | solution.py:202
  419.7 153.2 %all-gather.25.cloned.1.call-start = ((), (), s32[]{:S(2)}) async-start(), calls=%async_computation.28 | async-start | bytes 5242880 | tf_op jit(solution)/shard_map/all_gather | solution.py:81
  450.9 210.2 %reduce-scatter.24.cloned.1.call-start = ((), (), s32[]{:S(2)}) async-start(), calls=%async_computation.29 | async-start | bytes 9830400 | tf_op jit(solution)/shard_map/reduce_scatter | solution.py:96
  503.6 79.8 %copy-start.31 = (bf16[960,640]{1,0:T(8,128)(2,1)S(1)}, bf16[960,640]{1,0:T(8,128)(2,1)}, u32[]{:S(2)}) copy-start(bf16[960,640]{1,0:T(8,128)(2,1)} %all-gather.19.cloned.1.call-done) | copy-start | bytes 3686404
  583.4 3.3 copy-start.9
  583.4 3.3 copy-start.19
  592.1 69.0 %copy-start.3 = (f32[512,960]{0,1:T(8,128)S(1)}, f32[512,960]{0,1:T(8,128)}, u32[]{:S(2)}) copy-start(f32[512,960]{0,1:T(8,128)} %copy-done.2) | copy-start | bytes 5898244
  592.1 106.0 %all-gather.27.cloned.1.call-start = ((), (), s32[]{:S(2)}) async-start(), calls=%async_computation.30 | async-start | bytes 4915200 | tf_op jit(solution)/shard_map/all_gather | solution.py:81
  594.6 68.8 %copy-start.6 = (bf16[512,960]{0,1:T(8,128)(2,1)S(1)}, bf16[512,960]{0,1:T(8,128)(2,1)}, u32[]{:S(2)}) copy-start(bf16[512,960]{0,1:T(8,128)(2,1)} %copy.96) | copy-start | bytes 2949124
  702.4 17.2 %all-to-all-start.5 = ((bf16[4,512,240]{1,2,0:T(8,128)(2,1)}), bf16[4,512,240]{1,2,0:T(8,128)(2,1)S(1)}, u32[]{:S(2)}, u32[]{:S(2)}) async-start(bf16[4,512,240]{1,2,0:T(8,128)(2,1)} %bitcast.164), calls=%async_computation.8 | async-start | bytes 1966080 | tf_op jit(solution)/shard_map/all_to_all | solution.py:85
  705.9 283.1 %reduce-scatter.26.cloned.1.call-start = ((), (), s32[]{:S(2)}) async-start(), calls=%async_computation.31 | async-start | bytes 1638400 | tf_op jit(solution)/shard_map/reduce_scatter | solution.py:289
  962.3 56.0 %reduce-scatter.28.cloned.1.call-start = ((), (), s32[]{:S(2)}) async-start(), calls=%async_computation.32 | async-start | bytes 1638400 | tf_op jit(solution)/shard_map/reduce_scatter | solution.py:292
  963.7 153.6 %reduce-scatter.30.cloned.1.call-start = ((), (), s32[]{:S(2)}) async-start(), calls=%async_computation.33 | async-start | bytes 9830400 | tf_op jit(solution)/shard_map/reduce_scatter | solution.py:96
  1019.4 23.6 %copy-start.21 = (bf16[960,400]{0,1:T(8,128)(2,1)S(1)}, bf16[960,400]{0,1:T(8,128)(2,1)}, u32[]{:S(2)}) copy-start(bf16[960,400]{0,1:T(8,128)(2,1)} %reshape.338) | copy-start | bytes 2304004
  1048.4 140.5 %reduce-scatter.22.cloned.1.call-start = ((), (), s32[]{:S(2)}) async-start(), calls=%async_computation.27 | async-start | bytes 9830400 | tf_op jit(solution)/shard_map/reduce_scatter | solution.py:96
  1057.5 222.8 %reduce-scatter.34.cloned.1.call-start = ((), (), s32[]{:S(2)}) async-start(), calls=%async_computation.35 | async-start | bytes 2211840
  1064.2 290.7 %reduce-scatter.40.cloned.1.call-start = ((), (), s32[]{:S(2)}) async-start(), calls=%async_computation.38 | async-start | bytes 2764800
  1072.3 8.1 copy-start.10
  1072.3 355.8 %reduce-scatter.36.cloned.1.call-start = ((), (), s32[]{:S(2)}) async-start(), calls=%async_computation.36 | async-start | bytes 2764800
  1080.3 37.0 %copy-start.26 = (f32[960]{0:T(1024)S(1)}, f32[960]{0:T(1024)}, u32[]{:S(2)}) copy-start(f32[960]{0:T(1024)} %param.19) | copy-start | bytes 11524
  1080.4 37.0 %copy-start.28 = (f32[512]{0:T(512)S(1)}, f32[512]{0:T(512)}, u32[]{:S(2)}) copy-start(f32[512]{0:T(512)} %copy-done.27) | copy-start | bytes 6148
  1080.4 421.2 %reduce-scatter.38.cloned.1.call-start = ((), (), s32[]{:S(2)}) async-start(), calls=%async_computation.37 | async-start | bytes 2764800
  1087.2 30.1 %copy-start.1 = (f32[512,960]{0,1:T(8,128)S(1)}, f32[512,960]{0,1:T(8,128)}, u32[]{:S(2)}) copy-start(f32[512,960]{0,1:T(8,128)} %copy-done) | copy-start | bytes 5898244
  1087.2 101.6 %copy-start.7 = (bf16[512,960]{0,1:T(8,128)(2,1)S(1)}, bf16[512,960]{0,1:T(8,128)(2,1)}, u32[]{:S(2)}) copy-start(bf16[512,960]{0,1:T(8,128)(2,1)} %copy.96) | copy-start | bytes 2949124
  1193.6 8.0 copy-start.13
  1195.9 48.6 %copy-start.12 = (bf16[4,30,8,512]{3,2,0,1:T(8,128)(2,1)S(1)}, bf16[4,30,8,512]{3,2,0,1:T(8,128)(2,1)}, u32[]{:S(2)}) copy-start(bf16[4,30,8,512]{3,2,0,1:T(8,128)(2,1)} %copy-done.11) | copy-start | bytes 2949124
  1195.9 44.9 %all-to-all-start.7 = ((bf16[8,64,960]{2,1,0:T(8,128)(2,1)}), bf16[8,64,960]{2,1,0:T(8,128)(2,1)S(1)}, u32[]{:S(2)}, u32[]{:S(2)}) async-start(bf16[8,64,960]{2,1,0:T(8,128)(2,1)} %bitcast.42), calls=%async_computation.13 | async-start | bytes 2097152 | tf_op jit(solution)/shard_map/all_to_all | solution.py:322
  1240.8 81.6 %all-to-all-start.3 = ((bf16[8,64,960]{2,1,0:T(8,128)(2,1)}), bf16[8,64,960]{2,1,0:T(8,128)(2,1)S(1)}, u32[]{:S(2)}, u32[]{:S(2)}) async-start(bf16[8,64,960]{2,1,0:T(8,128)(2,1)} %bitcast.22), calls=%async_computation.5 | async-start | bytes 2097152 | tf_op jit(solution)/shard_map/all_to_all | solution.py:321
  1244.4 4.5 copy-start.33
  1244.4 323.7 %reduce-scatter.32.cloned.1.call-start = ((), (), s32[]{:S(2)}) async-start(), calls=%async_computation.34 | async-start | bytes 1105920 | tf_op jit(solution)/shard_map/reduce_scatter | solution.py:314
  (12 other events, 19.8 us)
Sparse Core Ops, SparseCore 0:
  48.8 32.0 all-gather.10
  116.5 16.2 all-gather.12
  134.9 18.1 all-gather.14
  343.6 70.1 reduce-scatter.19
  665.0 32.9 all-gather.26
  962.5 26.5 reduce-scatter.25
  991.7 26.5 reduce-scatter.27
Sparse Core Ops, SparseCore 1:
  346.1 42.9 all-gather.20
  418.4 32.8 all-gather.16
  453.6 41.7 all-gather.18
  497.7 40.4 all-gather.22
  539.8 33.0 all-gather.24
  592.2 68.8 reduce-scatter.23
  1048.4 68.9 reduce-scatter.29
  1119.9 68.8 reduce-scatter.21
  1192.2 88.1 reduce-scatter.33
  1285.0 69.8 reduce-scatter.39
  1359.3 68.7 reduce-scatter.35
  1432.8 68.7 reduce-scatter.37
  1505.7 62.3 reduce-scatter.31
where the time goes:
time: 1590 us; the launch traced here: 1580 us
  waiting for transfers between devices  799 us (50%)
  matrix products  335 us (21%)
  blocking collectives  191 us (12%)
  local copies, waits for them, and re-layouts  105 us (7%)
  loops' own time  59.9 us (4%)
  other arithmetic  47.7 us (3%)
  starting transfers between devices  21.8 us (1%)
  between operations  16.8 us (1%)
    reduce_scatter x4, waiting for transfers between devices, spread_sum(): return lax.psum_scatter(result, 'col', scatter_dimension=0, tiled=True)  235 us
    unnamed x24, waiting for transfers between devices  208 us
    dot_general x50, matrix products, matmul_nt(): lax.dot_general(left_mat, right_mat, (((1,), (1,)), ((), ())), preferred_...  134 us
    dot_general x35, matrix products, matmul(): return jnp.dot(left_mat, right_mat, preferred_element_type=jnp.float32)  113 us
    dot_general x34, matrix products, matmul_tn(): lax.dot_general(left_mat, right_mat, (((0,), (0,)), ((), ())), preferred_...  80.8 us
    all_gather x4, waiting for transfers between devices, gather_rows(): return lax.all_gather(values, 'col', axis=0, tiled=True)  68.1 us
    reduce_scatter x1, waiting for transfers between devices, on_device(): lax.psum_scatter(grad_out_part, 'row', scatter_dimension=0, tiled=True)  66.6 us
    psum x1, blocking collectives, on_device(): lax.psum((gain_one_part, gain_two_part), ('row', 'col'))  39.7 us
  transfers between devices with their start and end apart: 25, of which 21 were waited for; matrix products, arithmetic and copies ran while one was open for 6% of the time, Pallas kernels for 0%

commit v1 on v0

--- a/solution.py
+++ b/solution.py
@@ -12,6 +12,22 @@
 EPS = 1e-05
 NEG_FILL = -1e30
 THETA = 10000.0
+
+
+def swapped_with_each(array, axis, split, join):
+    ways, here = (lax.axis_size(axis), lax.axis_index(axis))
+    width = array.shape[split] // ways
+    dims = list(array.shape)
+    dims[split] = width
+    height = dims[join]
+    dims[join] = height * ways
+    full = jnp.zeros(dims, array.dtype)
+    for mask in range(ways):
+        part = lax.dynamic_slice_in_dim(array, (here ^ mask) * width, width, axis=split)
+        if mask:
+            part = lax.ppermute(part, axis, [(d, d ^ mask) for d in range(ways)])
+        full = lax.dynamic_update_slice_in_dim(full, part, (here ^ mask) * height, axis=join)
+    return full
 
 
 def matmul(left_mat, right_mat):
@@ -191,7 +207,7 @@
         out_cotangent.reshape(row_devices, block_rows, model_width), sender, axis=0
     ).reshape(own_rows, model_width)
     dealt_input, dealt_cot = (
-        lax.all_to_all(input_blocks, "row", split_axis=0, concat_axis=0, tiled=True),
+        swapped_with_each(input_blocks, "row", 0, 0),
         lax.all_to_all(cot_blocks, "row", split_axis=0, concat_axis=0, tiled=True),
     )
     qkv_mat, out_mat, gate_mat, up_mat, down_mat = (

time: 1590 us -> 1660 us (1.044)
  local copies, waits for them, and re-layouts: 105 us -> 163 us
  blocking collectives: 191 us -> 159 us
  matrix products: 335 us -> 352 us
    all_to_all x1, waiting for transfers between devices: 0.01 us -> 38 us  [on_device(): lax.all_to_all(layer_out, 'row', split_axis=0, concat_axis=0, tiled=True)]
    all_to_all x1, waiting for transfers between devices: 38 us -> 0.01 us  [on_device(): lax.all_to_all(input_grad.astype(jnp.bfloat16), 'row', split_axis=0, conc...]
    all_gather x1, waiting for transfers between devices: 35.7 us -> 0.02 us  [on_device(): lax.all_gather(w_gate, 'row', axis=0, tiled=True)]
    all_gather x1, waiting for transfers between devices: 0.02 us -> 35.6 us  [on_device(): lax.all_gather(w_up, 'row', axis=0, tiled=True)]
    all_to_all x1 -> x0, blocking collectives: 32.9 us -> none  [on_device(): lax.all_to_all(input_blocks, 'row', split_axis=0, concat_axis=0, tiled=True)]
    while x0 -> x30, local copies, waits for them, and re-layouts: none -> 29.7 us
    dynamic_update_slice x0 -> x8, local copies, waits for them, and re-layouts: none -> 26.3 us  [swapped_with_each(): lax.dynamic_update_slice_in_dim(full, part, (here ^ mask) * height, axis=...]
    dot_general x35, matrix products: 113 us -> 130 us  [matmul(): return jnp.dot(left_mat, right_mat, preferred_element_type=jnp.float32)]
  transfers between devices with their start and end apart: 25 -> 32, of which waited for: 21 -> 23; matrix products, arithmetic and copies ran while one was open for 6% -> 7% of each run, Pallas kernels for 0% -> 0%
where the time goes in v1:
time: 1660 us; the launch traced here: 1640 us
  waiting for transfers between devices  810 us (49%)
  matrix products  352 us (21%)
  local copies, waits for them, and re-layouts  163 us (10%)
  blocking collectives  159 us (10%)
  loops' own time  59.7 us (4%)
  other arithmetic  49.2 us (3%)
  starting transfers between devices  34.5 us (2%)
  between operations  17.3 us (1%)
    reduce_scatter x4, waiting for transfers between devices, spread_sum(): return lax.psum_scatter(result, 'col', scatter_dimension=0, tiled=True)  234 us
    unnamed x24, waiting for transfers between devices  207 us
    dot_general x50, matrix products, matmul_nt(): lax.dot_general(left_mat, right_mat, (((1,), (1,)), ((), ())), preferred_...  134 us
    dot_general x35, matrix products, matmul(): return jnp.dot(left_mat, right_mat, preferred_element_type=jnp.float32)  130 us
    dot_general x34, matrix products, matmul_tn(): lax.dot_general(left_mat, right_mat, (((0,), (0,)), ((), ())), preferred_...  80.5 us
    all_gather x4, waiting for transfers between devices, gather_rows(): return lax.all_gather(values, 'col', axis=0, tiled=True)  68.6 us
    reduce_scatter x1, waiting for transfers between devices, on_device(): lax.psum_scatter(grad_out_part, 'row', scatter_dimension=0, tiled=True)  66.6 us
    psum x1, blocking collectives, on_device(): lax.psum((gain_one_part, gain_two_part), ('row', 'col'))  39.7 us
  transfers between devices with their start and end apart: 32, of which 23 were waited for; matrix products, arithmetic and copies ran while one was open for 7% of the time, Pallas kernels for 0%

profile of v1, /device:TPU:0, one launch (start us, length us, event | category | flops | bytes accessed | tf_op | source)
XLA Modules:
  0.0 1644.8 jit_solution(13501893516415860685)
XLA Ops:
  28.3 6.6 collective-permute-done.1
  52.2 5.0 collective-permute-done.4
  69.0 33.5 %all-gather = bf16[8,120,400]{1,2,0:T(8,128)(2,1)S(1)} all-gather(bf16[1,120,400]{1,2,0:T(8,128)(2,1)S(1)} %bitcast.268), channel_id=1, replica_groups=mesh['row'=8,'col'=4] {'row'}, dimensions={0}, use_global_device_ids=true | all-gather | bytes 864000 | tf_op jit(solution)/shard_map/all_gather | solution.py:214
  104.0 4.0 convolution_convert_fusion
  113.4 20.3 %all-to-all-done = bf16[4,512,400]{1,2,0:T(8,128)(2,1)S(1)} async-done(((bf16[4,512,400]{1,2,0:T(8,128)(2,1)}), bf16[4,512,400]{1,2,0:T(8,128)(2,1)S(1)}, u32[]{:S(2)}, u32[]{:S(2)}) %all-to-all-start) | async-done | bytes 1638432 | tf_op jit(solution)/shard_map/all_to_all | solution.py:101
  140.2 13.6 all-gather.13.cloned.1.call-done
  157.6 16.0 all-gather.15.cloned.1.call-done
  177.4 193.3 %while.34 = (s32[]{:T(128)}, bf16[15,512,64]{1,2,0:T(8,128)(2,1)}, f32[15,512]{1,0:T(8,128)}, bf16[15,512,64]{2,1,0:T(8,128)(2,1)}, s32[15]{0:T(128)S(1)}, /*ind...) while((s32[]{:T(128)}, bf16[15,512,64]{1,2,0:T(8,128)(2,1)}, ...), condition=%wide.region_8.10_spmd.clone.clone, body=%wide.region_5.9_spmd.clone.sunk.clone | while | flops 279969280 | bytes 30704928 | solution.py:135
  225.1 3.9 fusion.139
  250.8 3.9 fusion.139
  276.6 3.9 fusion.139
  302.4 3.9 fusion.139
  374.3 31.5 %all_gather.37 = bf16[960,240]{1,0:T(8,128)(2,1)S(1)} all-gather(bf16[120,240]{1,0:T(8,128)(2,1)S(1)} %copy-done.23), channel_id=1, replica_groups=mesh['row'=8,'col'=4] {'row'}, dimensions={0}, use_global_device_ids=true | all-gather | bytes 518400 | tf_op jit(solution)/shard_map/all_gather | solution.py:215
  406.9 4.3 fusion.71
  411.8 69.7 %reduce-scatter.20.cloned.1.call-done = f32[512,960]{0,1:T(8,128)} async-done(((f32[2048,960]{0,1:T(8,128)}), f32[512,960]{0,1:T(8,128)}) %reduce-scatter.20.cloned.1.call-update) | async-done | bytes 1966096 | tf_op jit(solution)/shard_map/reduce_scatter | solution.py:112
  486.1 31.2 %all_to_all.94 = bf16[8,64,960]{2,1,0:T(8,128)(2,1)} all-to-all(bf16[8,64,960]{2,1,0:T(8,128)(2,1)S(1)} %copy-done.6), channel_id=1, replica_groups=mesh['row'=8,'col'=4] {'row'}, dimensions={0} | all-to-all | bytes 1966080 | tf_op jit(solution)/shard_map/all_to_all | solution.py:211
  517.8 8.3 fusion.61
  526.1 35.6 %all-gather.21.cloned.1.call-done = bf16[960,640]{1,0:T(8,128)(2,1)} async-done(((bf16[120,640]{1,0:T(8,128)(2,1)}), bf16[960,640]{1,0:T(8,128)(2,1)}) %all-gather.21.cloned.1.call-update) | async-done | bytes 1228816 | tf_op jit(solution)/shard_map/all_gather | solution.py:217
  561.7 8.4 fusion.62
  570.0 34.5 %all-gather.23.cloned.1.call-done = bf16[960,640]{1,0:T(8,128)(2,1)} async-done(((bf16[120,640]{1,0:T(8,128)(2,1)}), bf16[960,640]{1,0:T(8,128)(2,1)}) %all-gather.23.cloned.1.call-update) | async-done | bytes 1228816 | tf_op jit(solution)/shard_map/all_gather | solution.py:218
  604.5 34.7 %all-gather.25.cloned.1.call-done = bf16[2048,960]{1,0:T(8,128)(2,1)} async-done(((bf16[512,960]{1,0:T(8,128)(2,1)}), bf16[2048,960]{1,0:T(8,128)(2,1)}) %all-gather.25.cloned.1.call-update) | async-done | bytes 3932176 | tf_op jit(solution)/shard_map/all_gather | solution.py:97
  639.2 10.5 multiply_convert_fusion.1
  653.1 5.5 convolution_add_fusion.1
  661.1 66.5 %reduce-scatter.24.cloned.1.call-done = f32[512,960]{0,1:T(8,128)} async-done(((f32[2048,960]{0,1:T(8,128)}), f32[512,960]{0,1:T(8,128)}) %reduce-scatter.24.cloned.1.call-update) | async-done | bytes 1966096 | tf_op jit(solution)/shard_map/reduce_scatter | solution.py:112
  731.4 33.2 %all-gather.27.cloned.1.call-done = bf16[2048,960]{0,1:T(8,128)(2,1)} async-done(((bf16[512,960]{0,1:T(8,128)(2,1)}), bf16[2048,960]{0,1:T(8,128)(2,1)}) %all-gather.27.cloned.1.call-update) | async-done | bytes 3932176 | tf_op jit(solution)/shard_map/all_gather | solution.py:97
  772.4 13.7 all-to-all-done.4
  789.7 237.5 %while.35 = (s32[]{:T(128)}, f32[5,2048,64]{1,2,0:T(8,128)}, f32[5,2048,64]{1,2,0:T(8,128)}, f32[15,512,64]{1,2,0:T(8,128)}, s32[15]{0:T(128)S(1)}, /*index=5*/b...) while((s32[]{:T(128)}, f32[5,2048,64]{1,2,0:T(8,128)}, ...), condition=%wide.region_16.18_spmd.clone.clone, body=%wide.region_14.17_spmd.clone.sunk.clone | while | flops 684097024 | bytes 37774124 | solution.py:175
  1035.4 21.5 %reduce-scatter.26.cloned.1.call-done = bf16[512,320]{0,1:T(8,128)(2,1)} async-done(((bf16[2048,320]{0,1:T(8,128)(2,1)}), bf16[512,320]{0,1:T(8,128)(2,1)}) %reduce-scatter.26.cloned.1.call-update) | async-done | bytes 327696 | tf_op jit(solution)/shard_map/reduce_scatter | solution.py:305
  1058.2 28.1 %reduce-scatter.28.cloned.1.call-done = bf16[512,320]{0,1:T(8,128)(2,1)} async-done(((bf16[2048,320]{0,1:T(8,128)(2,1)}), bf16[512,320]{0,1:T(8,128)(2,1)}) %reduce-scatter.28.cloned.1.call-update) | async-done | bytes 327696 | tf_op jit(solution)/shard_map/reduce_scatter | solution.py:308
  1087.3 23.3 %all_to_all.95 = bf16[512,4,400]{0,2,1:T(8,128)(2,1)S(1)} all-to-all(bf16[512,4,400]{0,2,1:T(8,128)(2,1)S(1)} %bitcast.241), channel_id=1, replica_groups=mesh['row'=8,'col'=4] {'col'}, dimensions={1} | all-to-all | bytes 3276800 | tf_op jit(solution)/shard_map/all_to_all | solution.py:105
  1112.1 5.4 fusion.65
  1118.7 7.9 fusion.63
  1126.7 7.4 fusion.66
  1134.5 7.6 fusion.68
  1142.1 7.6 fusion.69
  1149.8 7.8 fusion.70
  1157.6 28.9 %reduce-scatter.30.cloned.1.call-done = f32[512,960]{0,1:T(8,128)} async-done(((f32[2048,960]{0,1:T(8,128)}), f32[512,960]{0,1:T(8,128)}) %reduce-scatter.30.cloned.1.call-update) | async-done | bytes 1966096 | tf_op jit(solution)/shard_map/reduce_scatter | solution.py:112
  1188.7 69.3 %reduce-scatter.22.cloned.1.call-done = f32[512,960]{0,1:T(8,128)} async-done(((f32[2048,960]{0,1:T(8,128)}), f32[512,960]{0,1:T(8,128)}) %reduce-scatter.22.cloned.1.call-update) | async-done | bytes 1966096 | tf_op jit(solution)/shard_map/reduce_scatter | solution.py:112
  1257.9 4.5 fusion.55
  1264.9 5.6 all-to-all-start.2
  1271.8 38.0 %all-to-all-done.2 = bf16[8,64,960]{2,1,0:T(8,128)(2,1)S(1)} async-done(((bf16[8,64,960]{2,1,0:T(8,128)(2,1)}), bf16[8,64,960]{2,1,0:T(8,128)(2,1)S(1)}, u32[]{:S(2)}, u32[]{:S(2)}) %all-to-all-start.2) | async-done | bytes 983072 | tf_op jit(solution)/shard_map/all_to_all | solution.py:337
  1313.4 4.4 fusion.67
  1317.9 31.9 %reduce-scatter.34.cloned.1.call-done = f32[120,400]{1,0:T(8,128)} async-done(((f32[960,400]{1,0:T(8,128)}), f32[120,400]{1,0:T(8,128)}) %reduce-scatter.34.cloned.1.call-update) | async-done | bytes 192016
  1351.6 39.7 %all-reduce.3 = (f32[960]{0:T(1024)}, f32[960]{0:T(1024)}) all-reduce(f32[960]{0:T(1024)S(1)} %get-tuple-element.467, f32[960]{0:T(1024)S(1)} %get-tuple-element.465), channel_id=1, replica_groups=mesh['row'=8,'col'=4] {'row','col'}, use_global_device_ids=true, to_apply=%region_22.24 | all-reduce | flops 1920 | bytes 15360 | tf_op jit(solution)/shard_map/psum | solution.py:335
  1397.4 26.1 %reduce-scatter.36.cloned.1.call-done = f32[120,640]{1,0:T(8,128)} async-done(((f32[960,640]{1,0:T(8,128)}), f32[120,640]{1,0:T(8,128)}) %reduce-scatter.36.cloned.1.call-update) | async-done | bytes 307216
  1423.5 73.3 %reduce-scatter.38.cloned.1.call-done = f32[120,640]{1,0:T(8,128)} async-done(((f32[960,640]{1,0:T(8,128)}), f32[120,640]{1,0:T(8,128)}) %reduce-scatter.38.cloned.1.call-update) | async-done | bytes 307216
  1496.8 73.4 %reduce-scatter.40.cloned.1.call-done = f32[120,640]{1,0:T(8,128)} async-done(((f32[960,640]{1,0:T(8,128)}), f32[120,640]{1,0:T(8,128)}) %reduce-scatter.40.cloned.1.call-update) | async-done | bytes 307216
  1570.2 66.6 %reduce-scatter.32.cloned.1.call-done = f32[120,240]{1,0:T(8,128)} async-done(((f32[960,240]{1,0:T(8,128)}), f32[120,240]{1,0:T(8,128)}) %reduce-scatter.32.cloned.1.call-update) | async-done | bytes 115216 | tf_op jit(solution)/shard_map/reduce_scatter | solution.py:330
  (469 shorter events, 487.5 us)
Async XLA Ops:
  8.0 96.0 %all-gather.11.cloned.1.call-start = ((), (), s32[]{:S(2)}) async-start(), calls=%async_computation.18 | async-start | bytes 4915200 | tf_op jit(solution)/shard_map/all_gather | solution.py:97
  13.8 10.9 collective-permute-start
  17.0 18.0 %collective-permute-start.1 = (bf16[64,960]{0,1:T(8,128)(2,1)S(1)}, bf16[64,960]{0,1:T(8,128)(2,1)S(1)}, u32[]{:S(2)}, u32[]{:S(2)}) collective-permute-start(bf16[64,960]{0,1:T(8,128)(2,1)S(1)} %copy.135), channel_id=1, source_target_pairs={{0,8},{4,12},{8,0},{12,4},{16,24},{20,28},{24,16},{28,20},{1,9},{5... | collective-permute-start | bytes 368648 | tf_op jit(solution)/shard_map/ppermute | solution.py:28
  19.5 26.2 %collective-permute-start.2 = (bf16[64,960]{0,1:T(8,128)(2,1)}, bf16[64,960]{0,1:T(8,128)(2,1)S(1)}, u32[]{:S(2)}, u32[]{:S(2)}) collective-permute-start(bf16[64,960]{0,1:T(8,128)(2,1)} %copy.136), channel_id=1, source_target_pairs={{0,12},{4,8},{8,4},{12,0},{16,28},{20,24},{24,20},{28,16},{1,13},{... | collective-permute-start | bytes 368648 | tf_op jit(solution)/shard_map/ppermute | solution.py:28
  19.7 29.7 %collective-permute-start.3 = (bf16[64,960]{0,1:T(8,128)(2,1)S(1)}, bf16[64,960]{0,1:T(8,128)(2,1)S(1)}, u32[]{:S(2)}, u32[]{:S(2)}) collective-permute-start(bf16[64,960]{0,1:T(8,128)(2,1)S(1)} %copy.137), channel_id=1, source_target_pairs={{0,16},{4,20},{8,24},{12,28},{16,0},{20,4},{24,8},{28,12},{1,17},{... | collective-permute-start | bytes 368648 | tf_op jit(solution)/shard_map/ppermute | solution.py:28
  22.9 34.3 %collective-permute-start.4 = (bf16[64,960]{0,1:T(8,128)(2,1)S(1)}, bf16[64,960]{0,1:T(8,128)(2,1)S(1)}, u32[]{:S(2)}, u32[]{:S(2)}) collective-permute-start(bf16[64,960]{0,1:T(8,128)(2,1)S(1)} %copy.138), channel_id=1, source_target_pairs={{0,20},{4,16},{8,28},{12,24},{16,4},{20,0},{24,12},{28,8},{1,21},{... | collective-permute-start | bytes 368648 | tf_op jit(solution)/shard_map/ppermute | solution.py:28
  24.7 36.1 %collective-permute-start.5 = (bf16[64,960]{0,1:T(8,128)(2,1)S(1)}, bf16[64,960]{0,1:T(8,128)(2,1)}, u32[]{:S(2)}, u32[]{:S(2)}) collective-permute-start(bf16[64,960]{0,1:T(8,128)(2,1)S(1)} %copy.139), channel_id=1, source_target_pairs={{0,24},{4,28},{8,16},{12,20},{16,8},{20,12},{24,0},{28,4},{1,25},{... | collective-permute-start | bytes 368648 | tf_op jit(solution)/shard_map/ppermute | solution.py:28
  35.0 28.8 %collective-permute-start.6 = (bf16[64,960]{0,1:T(8,128)(2,1)S(1)}, bf16[64,960]{0,1:T(8,128)(2,1)}, u32[]{:S(2)}, u32[]{:S(2)}) collective-permute-start(bf16[64,960]{0,1:T(8,128)(2,1)S(1)} %copy.140), channel_id=1, source_target_pairs={{0,28},{4,24},{8,20},{12,16},{16,12},{20,8},{24,4},{28,0},{1,29},{... | collective-permute-start | bytes 368648 | tf_op jit(solution)/shard_map/ppermute | solution.py:28
  35.9 31.8 %copy-start.24 = (f32[960]{0:T(1024)S(1)}, f32[960]{0:T(1024)}, u32[]{:S(2)}) copy-start(f32[960]{0:T(1024)} %param.19) | copy-start | bytes 11524
  52.2 16.8 %copy-start.21 = (bf16[120,400]{0,1:T(8,128)(2,1)S(1)}, bf16[120,400]{0,1:T(8,128)(2,1)}, u32[]{:S(2)}) copy-start(bf16[120,400]{0,1:T(8,128)(2,1)} %param.20) | copy-start | bytes 288004
  67.4 414.1 %copy-start.1 = (bf16[512,960]{0,1:T(8,128)(2,1)}, bf16[512,960]{0,1:T(8,128)(2,1)S(1)}, u32[]{:S(2)}) copy-start(bf16[512,960]{0,1:T(8,128)(2,1)S(1)} %dynamic_update_slice.64) | copy-start | bytes 2949124
  67.7 35.0 %copy-start.26 = (f32[512]{0:T(512)}, f32[512]{0:T(512)S(1)}, u32[]{:S(2)}) copy-start(f32[512]{0:T(512)S(1)} %add_rsqrt_fusion.1) | copy-start | bytes 6148
  109.4 24.3 %all-to-all-start = ((bf16[4,512,400]{1,2,0:T(8,128)(2,1)}), bf16[4,512,400]{1,2,0:T(8,128)(2,1)S(1)}, u32[]{:S(2)}, u32[]{:S(2)}) async-start(bf16[4,512,400]{1,2,0:T(8,128)(2,1)} %bitcast.240), calls=%async_computation | async-start | bytes 3276800 | tf_op jit(solution)/shard_map/all_to_all | solution.py:101
  113.0 23.3 %copy-start.31 = (s32[1,3]{1,0:T(1,128)S(1)}, s32[1,3]{1,0:T(1,128)}, u32[]{:S(2)}) copy-start(s32[1,3]{1,0:T(1,128)} %param.27) | copy-start | bytes 40
  113.0 40.8 %all-gather.13.cloned.1.call-start = ((), (), s32[]{:S(2)}) async-start(), calls=%async_computation.19 | async-start | bytes 1638400 | tf_op jit(solution)/shard_map/all_gather | solution.py:244
  113.4 24.6 %copy-start.11 = (f32[512,32]{0,1:T(8,128)}, f32[512,32]{0,1:T(8,128)S(1)}, u32[]{:S(2)}) copy-start(f32[512,32]{0,1:T(8,128)S(1)} %get-tuple-element.548) | copy-start | bytes 196612
  113.4 24.6 %copy-start.13 = (f32[512,32]{0,1:T(8,128)}, f32[512,32]{0,1:T(8,128)S(1)}, u32[]{:S(2)}) copy-start(f32[512,32]{0,1:T(8,128)S(1)} %get-tuple-element.549) | copy-start | bytes 196612
  135.5 38.1 %all-gather.15.cloned.1.call-start = ((), (), s32[]{:S(2)}) async-start(), calls=%async_computation.20 | async-start | bytes 1638400 | tf_op jit(solution)/shard_map/all_gather | solution.py:245
  177.4 196.8 %copy-start.23 = (bf16[120,240]{1,0:T(8,128)(2,1)S(1)}, bf16[120,240]{1,0:T(8,128)(2,1)}, u32[]{:S(2)}) copy-start(bf16[120,240]{1,0:T(8,128)(2,1)} %param.21) | copy-start | bytes 172804
  370.7 35.1 %all-to-all-start.1 = ((bf16[512,4,240]{0,2,1:T(8,128)(2,1)}), bf16[512,4,240]{0,2,1:T(8,128)(2,1)S(1)}, u32[]{:S(2)}, u32[]{:S(2)}) async-start(bf16[512,4,240]{0,2,1:T(8,128)(2,1)} %bitcast.20), calls=%async_computation.1 | async-start | bytes 1966080 | tf_op jit(solution)/shard_map/all_to_all | solution.py:105
  374.2 107.3 %reduce-scatter.20.cloned.1.call-start = ((), (), s32[]{:S(2)}) async-start(), calls=%async_computation.21 | async-start | bytes 9830400 | tf_op jit(solution)/shard_map/reduce_scatter | solution.py:112
  411.2 72.3 %copy-start.22 = (f32[960]{0:T(1024)S(1)}, f32[960]{0:T(1024)}, u32[]{:S(2)}) copy-start(f32[960]{0:T(1024)} %param.22) | copy-start | bytes 11524
  411.2 106.5 %all-gather.19.cloned.1.call-start = ((), (), s32[]{:S(2)}) async-start(), calls=%async_computation.23 | async-start | bytes 1382400 | tf_op jit(solution)/shard_map/all_gather | solution.py:216
  411.8 106.0 %all-gather.17.cloned.1.call-start = ((), (), s32[]{:S(2)}) async-start(), calls=%async_computation.22 | async-start | bytes 4915200 | tf_op jit(solution)/shard_map/all_gather | solution.py:97
  484.7 77.0 %all-gather.21.cloned.1.call-start = ((), (), s32[]{:S(2)}) async-start(), calls=%async_computation.24 | async-start | bytes 1382400 | tf_op jit(solution)/shard_map/all_gather | solution.py:217
  485.3 119.3 %all-gather.23.cloned.1.call-start = ((), (), s32[]{:S(2)}) async-start(), calls=%async_computation.25 | async-start | bytes 1382400 | tf_op jit(solution)/shard_map/all_gather | solution.py:218
  486.0 153.2 %all-gather.25.cloned.1.call-start = ((), (), s32[]{:S(2)}) async-start(), calls=%async_computation.27 | async-start | bytes 5242880 | tf_op jit(solution)/shard_map/all_gather | solution.py:97
  517.2 210.3 %reduce-scatter.24.cloned.1.call-start = ((), (), s32[]{:S(2)}) async-start(), calls=%async_computation.28 | async-start | bytes 9830400 | tf_op jit(solution)/shard_map/reduce_scatter | solution.py:112
  639.2 10.5 copy-start.30
  658.6 105.9 %all-gather.27.cloned.1.call-start = ((), (), s32[]{:S(2)}) async-start(), calls=%async_computation.29 | async-start | bytes 4915200 | tf_op jit(solution)/shard_map/all_gather | solution.py:97
  661.1 68.8 %copy-start.5 = (bf16[512,960]{0,1:T(8,128)(2,1)S(1)}, bf16[512,960]{0,1:T(8,128)(2,1)}, u32[]{:S(2)}) copy-start(bf16[512,960]{0,1:T(8,128)(2,1)} %copy.120) | copy-start | bytes 2949124
  768.9 17.2 %all-to-all-start.4 = ((bf16[4,512,240]{1,2,0:T(8,128)(2,1)}), bf16[4,512,240]{1,2,0:T(8,128)(2,1)S(1)}, u32[]{:S(2)}, u32[]{:S(2)}) async-start(bf16[4,512,240]{1,2,0:T(8,128)(2,1)} %bitcast.163), calls=%async_computation.7 | async-start | bytes 1966080 | tf_op jit(solution)/shard_map/all_to_all | solution.py:101
  772.4 284.6 %reduce-scatter.26.cloned.1.call-start = ((), (), s32[]{:S(2)}) async-start(), calls=%async_computation.30 | async-start | bytes 1638400 | tf_op jit(solution)/shard_map/reduce_scatter | solution.py:305
  1030.3 55.9 %reduce-scatter.28.cloned.1.call-start = ((), (), s32[]{:S(2)}) async-start(), calls=%async_computation.31 | async-start | bytes 1638400 | tf_op jit(solution)/shard_map/reduce_scatter | solution.py:308
  1033.5 153.0 %reduce-scatter.30.cloned.1.call-start = ((), (), s32[]{:S(2)}) async-start(), calls=%async_computation.32 | async-start | bytes 9830400 | tf_op jit(solution)/shard_map/reduce_scatter | solution.py:112
  1087.3 24.8 %copy-start.19 = (bf16[960,400]{0,1:T(8,128)(2,1)S(1)}, bf16[960,400]{0,1:T(8,128)(2,1)}, u32[]{:S(2)}) copy-start(bf16[960,400]{0,1:T(8,128)(2,1)} %copy-done.18) | copy-start | bytes 2304004
  1117.5 140.5 %reduce-scatter.22.cloned.1.call-start = ((), (), s32[]{:S(2)}) async-start(), calls=%async_computation.26 | async-start | bytes 9830400 | tf_op jit(solution)/shard_map/reduce_scatter | solution.py:112
  1126.7 223.1 %reduce-scatter.34.cloned.1.call-start = ((), (), s32[]{:S(2)}) async-start(), calls=%async_computation.34 | async-start | bytes 2211840
  1134.1 289.4 %reduce-scatter.36.cloned.1.call-start = ((), (), s32[]{:S(2)}) async-start(), calls=%async_computation.35 | async-start | bytes 2764800
  1142.1 354.7 %reduce-scatter.38.cloned.1.call-start = ((), (), s32[]{:S(2)}) async-start(), calls=%async_computation.36 | async-start | bytes 2764800
  1149.7 36.7 %copy-start.25 = (f32[960]{0:T(1024)S(1)}, f32[960]{0:T(1024)}, u32[]{:S(2)}) copy-start(f32[960]{0:T(1024)} %param.19) | copy-start | bytes 11524
  1149.8 36.7 %copy-start.27 = (f32[512]{0:T(512)S(1)}, f32[512]{0:T(512)}, u32[]{:S(2)}) copy-start(f32[512]{0:T(512)} %copy-done.26) | copy-start | bytes 6148
  1149.8 420.4 %reduce-scatter.40.cloned.1.call-start = ((), (), s32[]{:S(2)}) async-start(), calls=%async_computation.37 | async-start | bytes 2764800
  1157.6 28.9 %copy-start.2 = (bf16[512,960]{0,1:T(8,128)(2,1)S(1)}, bf16[512,960]{0,1:T(8,128)(2,1)}, u32[]{:S(2)}) copy-start(bf16[512,960]{0,1:T(8,128)(2,1)} %copy-done.1) | copy-start | bytes 2949124
  1264.9 48.6 %copy-start.9 = (bf16[4,30,8,512]{3,2,0,1:T(8,128)(2,1)S(1)}, bf16[4,30,8,512]{3,2,0,1:T(8,128)(2,1)}, u32[]{:S(2)}) copy-start(bf16[4,30,8,512]{3,2,0,1:T(8,128)(2,1)} %copy-done.8) | copy-start | bytes 2949124
  1264.9 44.9 %all-to-all-start.2 = ((bf16[8,64,960]{2,1,0:T(8,128)(2,1)}), bf16[8,64,960]{2,1,0:T(8,128)(2,1)S(1)}, u32[]{:S(2)}, u32[]{:S(2)}) async-start(bf16[8,64,960]{2,1,0:T(8,128)(2,1)} %bitcast.22), calls=%async_computation.4 | async-start | bytes 2097152 | tf_op jit(solution)/shard_map/all_to_all | solution.py:337
  1309.8 82.1 %all-to-all-start.6 = ((bf16[8,64,960]{2,1,0:T(8,128)(2,1)}), bf16[8,64,960]{2,1,0:T(8,128)(2,1)S(1)}, u32[]{:S(2)}, u32[]{:S(2)}) async-start(bf16[8,64,960]{2,1,0:T(8,128)(2,1)} %bitcast.42), calls=%async_computation.12 | async-start | bytes 2097152 | tf_op jit(solution)/shard_map/all_to_all | solution.py:338
  1313.4 323.4 %reduce-scatter.32.cloned.1.call-start = ((), (), s32[]{:S(2)}) async-start(), calls=%async_computation.33 | async-start | bytes 1105920 | tf_op jit(solution)/shard_map/reduce_scatter | solution.py:330
  (32 other events, 80.9 us)
Sparse Core Ops, SparseCore 0:
  69.1 34.9 all-gather.10
  135.6 18.1 all-gather.12
  155.4 18.1 all-gather.14
  411.3 70.1 reduce-scatter.19
  731.5 32.9 all-gather.26
  1030.4 26.5 reduce-scatter.25
  1059.7 26.5 reduce-scatter.27
Sparse Core Ops, SparseCore 1:
  413.8 42.8 all-gather.18
  484.8 32.8 all-gather.16
  519.9 41.7 all-gather.20
  564.1 40.4 all-gather.22
  606.2 33.0 all-gather.24
  658.7 68.8 reduce-scatter.23
  1117.6 68.9 reduce-scatter.29
  1189.0 68.8 reduce-scatter.21
  1261.3 88.4 reduce-scatter.33
  1354.5 69.0 reduce-scatter.35
  1428.0 68.7 reduce-scatter.37
  1501.5 68.7 reduce-scatter.39
  1574.4 62.4 reduce-scatter.31
